TPU v7x, 32 devices: a whole 2x2x4 slice. The times are simulated.
32 devices in a mesh: dp: 8 (over z, x), expert: 4 (over y, core).
Axes of the slice: x: 2, y: 2, z: 4, core: 2. Of those that a mesh axis runs over, the one named last changes fastest.
Arguments:
- tokens: bfloat16 [6272, 768], P(('dp', 'expert')), may hold values from -6 to 6
- counts: int32 [32, 2], P(('dp', 'expert')), may hold values from 0 to 4, as said below
- routes: int32 [6272, 2], P(('dp', 'expert')), may hold values from 0 to 31, all different within a row
- priority: int32 [32, 196], P(('dp', 'expert')), may hold values from 0 to 195, each once within a row
- out_grad: bfloat16 [6272, 768], P(('dp', 'expert')), may hold values from -6 to 6
- pre_gain: bfloat16 [768], P(('dp', 'expert')), may hold values from 0.5 to 1.5
- pre_shift: bfloat16 [768], P(('dp', 'expert')), may hold values from -1.5 to 1.5
- w_qkv: bfloat16 [768, 2304], P(('dp', 'expert')), may hold values from -0.21875 to 0.21875
- w_out: bfloat16 [768, 768], P(('dp', 'expert')), may hold values from -0.625 to 0.625
- moe_gain: bfloat16 [768], P(('dp', 'expert')), may hold values from 0.5 to 1.5
- moe_shift: bfloat16 [768], P(('dp', 'expert')), may hold values from -1.5 to 1.5
- w_router: bfloat16 [768, 32], P(('dp', 'expert')), may hold values from -0.15625 to 0.15625
- w_up: bfloat16 [32, 768, 3072], P('expert', 'dp'), may hold values from -0.21875 to 0.21875
- w_down: bfloat16 [32, 3072, 768], P('expert', 'dp'), may hold values from -0.109375 to 0.109375
Outputs:
- out_tokens: bfloat16 [6272, 768], P(('dp', 'expert'))
- d_tokens: float32 [6272, 768], P(('dp', 'expert'))
- d_pre_gain: float32 [768], P(('dp', 'expert'))
- d_pre_shift: float32 [768], P(('dp', 'expert'))
- d_w_qkv: float32 [768, 2304], P(('dp', 'expert'))
- d_w_out: float32 [768, 768], P(('dp', 'expert'))
- d_moe_gain: float32 [768], P(('dp', 'expert'))
- d_moe_shift: float32 [768], P(('dp', 'expert'))
- d_w_router: float32 [768, 32], P(('dp', 'expert'))
- d_w_up: float32 [32, 768, 3072], P('expert', 'dp')
- d_w_down: float32 [32, 3072, 768], P('expert', 'dp')
Inputs may be any that keep to these rules, and one draw needn't show every extreme that they name: counts[s,0] is the number of large images (196 patches) and counts[s,1] of small ones (49 patches) of shard s, laid from the shard's first row, large ones first; counts[s,1] = (196 - 196 counts[s,0]) // 49; counts[s,0] is at most 1. `routes`: the two experts of a row differ. Each row of priority names every rank once; lower ranks take slots first.
All inputs are finite; a program needn't handle non-finite values.
Results may differ from a plain program's by a relative error of at most 0.014.
Values may be sent and summed in bfloat16 or wider, within the bound.
A program may use at most 320 MiB of HBM per device.

v0:
```python
from functools import partial
import math
import jax
import jax.numpy as jnp
from jax import lax
from jax.sharding import PartitionSpec as P

D = 768
HEADS = 12
HEAD_DIM = 64
EXPERTS = 32
PATCH_S = 49
PATCH_L = 196
CAP = 13


def normalize(inputs, scale_vec, shift_vec):
    average = jnp.mean(inputs, axis=-1, keepdims=True)
    centred = inputs - average
    variance = jnp.mean(centred * centred, axis=-1, keepdims=True)
    return centred * lax.rsqrt(variance + 1e-06) * scale_vec + shift_vec


def slot_numbers(chosen, rank_of, usable):
    earlier = (rank_of[:, None] < rank_of[None, :]) & usable[:, None]
    first_ids = chosen[:, 0]
    second_ids = chosen[:, 1]
    slot_first = jnp.sum(
        (earlier & (first_ids[:, None] == first_ids[None, :])).astype(jnp.int32), axis=0
    )
    crossing = usable[:, None] & (first_ids[:, None] == second_ids[None, :])
    slot_second = jnp.sum(
        (earlier & (second_ids[:, None] == second_ids[None, :])).astype(jnp.int32), axis=0
    )
    slot_second = slot_second + jnp.sum(crossing.astype(jnp.int32), axis=0)
    return jnp.stack([slot_first, slot_second], axis=1)


def block_probs(query_blk, seg_blk, key_rows, segment_ids):
    raw_scores = jnp.einsum("qhc,khc->hqk", query_blk, key_rows, preferred_element_type=jnp.float32)
    same_seg = (seg_blk[:, None] == segment_ids[None, :])[None]
    return jax.nn.softmax(
        jnp.where(same_seg, raw_scores * (1.0 / math.sqrt(HEAD_DIM)), -1e30), axis=-1
    )


def body(
    tokens,
    counts,
    routes,
    priority,
    out_grad,
    pre_gain,
    pre_shift,
    w_qkv,
    w_out,
    moe_gain,
    moe_shift,
    w_router,
    w_up,
    w_down,
):
    every = ("dp", "expert")
    dense = lax.all_gather(
        jnp.concatenate(
            [w_qkv, w_out, w_router]
            + [vector[:, None] for vector in (pre_gain, pre_shift, moe_gain, moe_shift)],
            axis=1,
        ),
        every,
        axis=0,
        tiled=True,
    )
    edges = (3 * D, 4 * D, 4 * D + EXPERTS)
    qkv_full, outp_full, router_full = (
        dense[:, : edges[0]],
        dense[:, edges[0] : edges[1]],
        dense[:, edges[1] : edges[2]],
    )
    gain_one, shift_one, gain_two, shift_two = (dense[:, edges[2] + i] for i in range(4))
    up_slice = lax.all_to_all(w_up, "dp", split_axis=2, concat_axis=1, tiled=True)
    row_count = tokens.shape[0]
    scale_factor = 1.0 / math.sqrt(HEAD_DIM)
    positions = jnp.arange(row_count, dtype=jnp.int32)
    large_count = counts[0, 0]
    small_count = counts[0, 1]
    large_end = large_count * PATCH_L
    used_end = large_end + small_count * PATCH_S
    segment_ids = jnp.where(
        positions < large_end,
        positions // PATCH_L,
        jnp.where(positions < used_end, large_count + (positions - large_end) // PATCH_S, -1),
    )
    usable = positions < used_end
    rows_in = tokens.astype(jnp.float32)
    normed_one, pull_one = jax.vjp(
        normalize, rows_in, gain_one.astype(jnp.float32), shift_one.astype(jnp.float32)
    )
    packed_one = normed_one.astype(jnp.bfloat16)
    projected = jnp.dot(packed_one, qkv_full, preferred_element_type=jnp.float32).astype(
        jnp.bfloat16
    )
    queries = projected[:, :D].reshape(row_count, HEADS, HEAD_DIM)
    key_rows = projected[:, D : 2 * D].reshape(row_count, HEADS, HEAD_DIM)
    value_rows = projected[:, 2 * D :].reshape(row_count, HEADS, HEAD_DIM)
    blocks = row_count // PATCH_L
    query_blocks = queries.reshape(blocks, PATCH_L, HEADS, HEAD_DIM)
    seg_blocks = segment_ids.reshape(blocks, PATCH_L)

    def forward_block(operands):
        attn_probs = block_probs(operands[0], operands[1], key_rows, segment_ids)
        return jnp.einsum(
            "hqk,khc->qhc",
            attn_probs.astype(jnp.bfloat16),
            value_rows,
            preferred_element_type=jnp.float32,
        ).astype(jnp.bfloat16)

    mixed_rows = lax.map(forward_block, (query_blocks, seg_blocks)).reshape(row_count, D)
    middle = rows_in + jnp.dot(mixed_rows, outp_full, preferred_element_type=jnp.float32)
    normed_two, pull_two = jax.vjp(
        normalize, middle, gain_two.astype(jnp.float32), shift_two.astype(jnp.float32)
    )
    packed_two = normed_two.astype(jnp.bfloat16)
    router_f32 = router_full.astype(jnp.float32)
    packed_f32 = packed_two.astype(jnp.float32)
    logits = jnp.dot(packed_two, router_full, preferred_element_type=jnp.float32)
    expert_ids = jnp.arange(EXPERTS, dtype=jnp.int32)
    onehot = routes[:, :, None] == expert_ids[None, None, :]
    picked = jnp.sum(jnp.where(onehot, logits[:, None, :], 0.0), axis=2)
    gate_vals = jax.nn.softmax(picked, axis=-1)
    slot_ids = slot_numbers(routes, priority[0], usable)
    kept_mask = usable[:, None] & (slot_ids < CAP)
    slot_total = EXPERTS * CAP
    flat_dest = jnp.where(kept_mask, routes * CAP + slot_ids, slot_total)
    token_of_slot = (
        jnp.full((slot_total + 1,), row_count, jnp.int32)
        .at[flat_dest.reshape(-1)]
        .set(jnp.repeat(positions, 2))
    )
    token_of_slot = token_of_slot[:slot_total]
    padded_rows = jnp.concatenate([packed_two, jnp.zeros((1, D), jnp.bfloat16)], axis=0)
    send_rows = jnp.take(padded_rows, token_of_slot, axis=0).reshape(EXPERTS, CAP, D)
    arrived = lax.all_to_all(send_rows, "expert", split_axis=0, concat_axis=1, tiled=True)
    arrived = lax.all_gather(arrived, "dp", axis=1, tiled=True)
    hidden = jnp.einsum("erd,edf->erf", arrived, up_slice, preferred_element_type=jnp.float32)
    activated, gelu_pull = jax.vjp(partial(jax.nn.gelu, approximate=False), hidden)
    activated = activated.astype(jnp.bfloat16)
    produced = jnp.einsum(
        "erf,efd->erd", activated, w_down, preferred_element_type=jnp.float32
    ).astype(jnp.bfloat16)
    produced = lax.psum_scatter(produced, "dp", scatter_dimension=1, tiled=True)
    returned = lax.all_to_all(produced, "expert", split_axis=1, concat_axis=0, tiled=True)
    flat_back = jnp.concatenate(
        [returned.reshape(slot_total, D), jnp.zeros((1, D), jnp.bfloat16)], axis=0
    )
    first_back = jnp.take(flat_back, flat_dest[:, 0], axis=0).astype(jnp.float32)
    second_back = jnp.take(flat_back, flat_dest[:, 1], axis=0).astype(jnp.float32)
    result = middle + gate_vals[:, 0:1] * first_back + gate_vals[:, 1:2] * second_back
    out_tokens = result.astype(jnp.bfloat16)
    grad_rows = out_grad.astype(jnp.float32)
    gate_grad = jnp.stack(
        [jnp.sum(grad_rows * first_back, axis=1), jnp.sum(grad_rows * second_back, axis=1)], axis=1
    )
    picked_grad = gate_vals * (gate_grad - jnp.sum(gate_vals * gate_grad, axis=1, keepdims=True))
    logit_grad = jnp.sum(jnp.where(onehot, picked_grad[:, :, None], 0.0), axis=1)
    slot_gate = (
        jnp.zeros((slot_total + 1,), jnp.float32)
        .at[flat_dest.reshape(-1)]
        .set(gate_vals.reshape(-1))
    )
    grad_pad = jnp.concatenate([grad_rows, jnp.zeros((1, D), jnp.float32)], axis=0)
    grad_send = (jnp.take(grad_pad, token_of_slot, axis=0) * slot_gate[:slot_total, None]).astype(
        jnp.bfloat16
    )
    grad_arrived = lax.all_to_all(
        grad_send.reshape(EXPERTS, CAP, D), "expert", split_axis=0, concat_axis=1, tiled=True
    )
    grad_arrived = lax.all_gather(grad_arrived, "dp", axis=1, tiled=True)
    down_share = jnp.einsum(
        "erf,erd->efd", activated, grad_arrived, preferred_element_type=jnp.float32
    )
    acted_grad = jnp.einsum(
        "erd,efd->erf", grad_arrived, w_down, preferred_element_type=jnp.float32
    )
    hidden_grad = gelu_pull(acted_grad)[0].astype(jnp.bfloat16)
    up_grad = jnp.einsum("erd,erf->edf", arrived, hidden_grad, preferred_element_type=jnp.float32)
    up_share = lax.all_to_all(
        up_grad.astype(jnp.bfloat16), "dp", split_axis=1, concat_axis=2, tiled=True
    ).astype(jnp.float32)
    input_grad = jnp.einsum(
        "erf,edf->erd", hidden_grad, up_slice, preferred_element_type=jnp.float32
    ).astype(jnp.bfloat16)
    input_grad = lax.psum_scatter(input_grad, "dp", scatter_dimension=1, tiled=True)
    back_grad = lax.all_to_all(input_grad, "expert", split_axis=1, concat_axis=0, tiled=True)
    flat_grad = jnp.concatenate(
        [back_grad.reshape(slot_total, D), jnp.zeros((1, D), jnp.bfloat16)], axis=0
    )
    normed_two_grad = jnp.take(flat_grad, flat_dest[:, 0], axis=0).astype(jnp.float32)
    normed_two_grad = normed_two_grad + jnp.take(flat_grad, flat_dest[:, 1], axis=0).astype(
        jnp.float32
    )
    normed_two_grad = normed_two_grad + jnp.einsum(
        "te,de->td", logit_grad, router_f32, precision=lax.Precision.HIGHEST
    )
    router_grad = jnp.einsum("td,te->de", packed_f32, logit_grad, precision=lax.Precision.HIGHEST)
    middle_part, gain_two_grad, shift_two_grad = pull_two(normed_two_grad)
    middle_grad = grad_rows + middle_part
    branch_grad = middle_grad.astype(jnp.bfloat16)
    out_proj_grad = jnp.einsum(
        "td,te->de", mixed_rows, branch_grad, preferred_element_type=jnp.float32
    )
    mixed_grad = jnp.einsum(
        "te,de->td", branch_grad, outp_full, preferred_element_type=jnp.float32
    ).astype(jnp.bfloat16)
    grad_blocks = mixed_grad.reshape(blocks, PATCH_L, HEADS, HEAD_DIM)

    def backward_block(carried, operands):
        key_acc, value_acc = carried
        query_blk, seg_blk, grad_blk = operands
        attn_probs = block_probs(query_blk, seg_blk, key_rows, segment_ids)
        probs_grad = jnp.einsum(
            "qhc,khc->hqk", grad_blk, value_rows, preferred_element_type=jnp.float32
        )
        value_acc = value_acc + jnp.einsum(
            "hqk,qhc->khc",
            attn_probs.astype(jnp.bfloat16),
            grad_blk,
            preferred_element_type=jnp.float32,
        )
        score_grad = attn_probs * (
            probs_grad - jnp.sum(attn_probs * probs_grad, axis=-1, keepdims=True)
        )
        raw_grad = (score_grad * scale_factor).astype(jnp.bfloat16)
        query_grad = jnp.einsum(
            "hqk,khc->qhc", raw_grad, key_rows, preferred_element_type=jnp.float32
        )
        key_acc = key_acc + jnp.einsum(
            "hqk,qhc->khc", raw_grad, query_blk, preferred_element_type=jnp.float32
        )
        return ((key_acc, value_acc), query_grad)

    zero_heads = jnp.zeros((row_count, HEADS, HEAD_DIM), jnp.float32)
    (key_grad, value_grad), query_grads = lax.scan(
        backward_block, (zero_heads, zero_heads), (query_blocks, seg_blocks, grad_blocks)
    )
    projected_grad = jnp.concatenate(
        [
            query_grads.reshape(row_count, D),
            key_grad.reshape(row_count, D),
            value_grad.reshape(row_count, D),
        ],
        axis=1,
    ).astype(jnp.bfloat16)
    qkv_grad = jnp.einsum(
        "td,te->de", packed_one, projected_grad, preferred_element_type=jnp.float32
    )
    normed_one_grad = jnp.einsum(
        "te,de->td", projected_grad, qkv_full, preferred_element_type=jnp.float32
    )
    rows_part, gain_one_grad, shift_one_grad = pull_one(normed_one_grad)
    tokens_grad = middle_grad + rows_part
    dense_grad = jnp.concatenate(
        [qkv_grad, out_proj_grad, router_grad]
        + [
            vector[:, None]
            for vector in (gain_one_grad, shift_one_grad, gain_two_grad, shift_two_grad)
        ],
        axis=1,
    ).astype(jnp.bfloat16)
    dense_share = lax.psum_scatter(dense_grad, every, scatter_dimension=0, tiled=True).astype(
        jnp.float32
    )
    return (
        out_tokens,
        tokens_grad,
        dense_share[:, edges[2]],
        dense_share[:, edges[2] + 1],
        dense_share[:, : edges[0]],
        dense_share[:, edges[0] : edges[1]],
        dense_share[:, edges[2] + 2],
        dense_share[:, edges[2] + 3],
        dense_share[:, edges[1] : edges[2]],
        up_share,
        down_share,
    )


def solution(mesh):
    placed = (
        P(("dp", "expert"), None),
        P(("dp", "expert"), None),
        P(("dp", "expert"), None),
        P(("dp", "expert"), None),
        P(("dp", "expert"), None),
        P(("dp", "expert")),
        P(("dp", "expert")),
        P(("dp", "expert"), None),
        P(("dp", "expert"), None),
        P(("dp", "expert")),
        P(("dp", "expert")),
        P(("dp", "expert"), None),
        P("expert", "dp", None),
        P("expert", "dp", None),
    )
    return jax.shard_map(
        body,
        mesh=mesh,
        in_specs=placed,
        out_specs=(
            P(("dp", "expert"), None),
            P(("dp", "expert"), None),
            P(("dp", "expert")),
            P(("dp", "expert")),
            P(("dp", "expert"), None),
            P(("dp", "expert"), None),
            P(("dp", "expert")),
            P(("dp", "expert")),
            P(("dp", "expert"), None),
            P("expert", "dp", None),
            P("expert", "dp", None),
        ),
        check_vma=False,
    )
```

profile of v0, /device:TPU:0, one launch (start us, length us, event | category | flops | bytes accessed | tf_op | source)
XLA Modules:
  0.0 902.9 jit_solution(15943545236240041457)
XLA Ops:
  24.0 55.0 %all-gather.4.cloned.1.call-done = bf16[768,3108]{1,0:T(8,128)(2,1)} async-done(((bf16[24,3108]{1,0:T(8,128)(2,1)}), bf16[768,3108]{1,0:T(8,128)(2,1)}) %all-gather.4.cloned.1.call-update) | async-done | bytes 4773904 | tf_op jit(solution)/shard_map/all_gather | solution.py:64
  95.7 14.2 %all_to_all.93 = bf16[32,13,768]{2,1,0:T(8,128)(2,1)S(1)} all-to-all(bf16[32,13,768]{2,1,0:T(8,128)(2,1)S(1)} %broadcast_select_fusion), channel_id=1, replica_groups=mesh['dp'=8,'expert'=4] {'expert'}, dimensions={0} | all-to-all | bytes 1277952 | tf_op jit(solution)/shard_map/all_to_all | solution.py:144
  111.0 8.6 copy.170
  119.6 198.4 %all_to_all.94 = bf16[8,96,3072]{1,0,2:T(8,128)(2,1)} all-to-all(bf16[8,96,3072]{1,0,2:T(8,128)(2,1)} %copy.170), channel_id=1, replica_groups=mesh['dp'=8,'expert'=4] {'dp'}, dimensions={2} | all-to-all | bytes 9437184 | tf_op jit(solution)/shard_map/all_to_all | solution.py:81
  318.0 8.5 copy.171
  326.5 8.4 fusion.35
  335.0 12.4 %multiply_convert_fusion = (bf16[8,416,384]{2,1,0:T(8,128)(2,1)S(1)}, f32[8,416,384]{2,1,0:T(8,128)}) fusion(f32[8,416,384]{2,1,0:T(8,128)S(1)} %get-tuple-element.109, u8[416,384]{1,0:T(8,128)(4,1)S(1)} %get-tuple-element.54, u8[416,384]{1,0:T(8,128)(4,1)S(1)} %get-tuple-element.53), kind=kLoop, calls=%fused_computation.19 | loop fusion | flops 89456640 | bytes 13099008 | tf_op jit(solution)/shard_map/convert_element_type | solution.py:148
  347.3 5.4 convolution_convert_fusion.3
  358.0 100.1 %reduce-scatter.6.cloned.1.call-done = bf16[8,52,768]{2,0,1:T(8,128)(2,1)} async-done(((bf16[8,416,768]{2,0,1:T(8,128)(2,1)}), bf16[8,52,768]{2,0,1:T(8,128)(2,1)}) %reduce-scatter.6.cloned.1.call-update) | async-done | bytes 638992 | tf_op jit(solution)/shard_map/reduce_scatter | solution.py:152
  488.5 14.0 %all_to_all.95 = bf16[32,13,768]{2,1,0:T(8,128)(2,1)S(1)} all-to-all(bf16[32,13,768]{2,1,0:T(8,128)(2,1)S(1)} %multiply_convert_fusion.2), channel_id=1, replica_groups=mesh['dp'=8,'expert'=4] {'expert'}, dimensions={0} | all-to-all | bytes 1277952 | tf_op jit(solution)/shard_map/all_to_all | solution.py:176
  503.7 83.1 %all-gather.8.cloned.1.call-done = bf16[8,416,768]{2,0,1:T(8,128)(2,1)} async-done(((bf16[8,52,768]{2,0,1:T(8,128)(2,1)}), bf16[8,416,768]{2,0,1:T(8,128)(2,1)}) %all-gather.8.cloned.1.call-update) | async-done | bytes 5111824 | tf_op jit(solution)/shard_map/all_gather | solution.py:179
  586.7 10.9 %add_convert_fusion = bf16[8,416,384]{2,1,0:T(8,128)(2,1)S(1)} fusion(f32[8,416,384]{2,1,0:T(8,128)} %get-tuple-element.90, f32[8,416,384]{2,1,0:T(8,128)} %copy-done.1, bf16[8,384,768]{2,1,0:T(8,128)(2,1)} %param.29, bf16[8,416,768]{2,0,1:T(8,128)(2,1)} %all-gather.8.cloned.1.call-done), kind=kOutput, calls=%fused_computation.18 | convolution fusion | flops 1980825600 | bytes 22609920 | tf_op jit(solution)/shard_map/erd,efd->erf/dot_general | solution.py:183
  597.6 6.9 convolution_convert_fusion.2
  604.5 5.2 copy.179
  612.4 96.9 %reduce-scatter.8.cloned.1.call-done = bf16[8,52,768]{2,0,1:T(8,128)(2,1)} async-done(((bf16[8,416,768]{2,0,1:T(8,128)(2,1)}), bf16[8,52,768]{2,0,1:T(8,128)(2,1)}) %reduce-scatter.8.cloned.1.call-update) | async-done | bytes 638992 | tf_op jit(solution)/shard_map/reduce_scatter | solution.py:194
  713.2 6.8 fusion.19
  751.8 5.6 fusion.39
  757.4 5.6 fusion.36
  778.2 8.7 concatenate.33
  787.0 9.3 %fusion.8 = f32[8,384,768]{2,1,0:T(8,128)} fusion(bf16[8,416,384]{2,1,0:T(8,128)(2,1)S(1)} %get-tuple-element.89, bf16[8,416,768]{2,0,1:T(8,128)(2,1)} %all-gather.8.cloned.1.call-done), kind=kOutput, calls=%fused_computation.33 | convolution fusion | flops 1962934272 | bytes 17104896 | tf_op jit(solution)/shard_map/erf,erd->efd/dot_general | solution.py:180
  796.3 43.3 %all-to-all-done.5 = bf16[8,768,384]{2,0,1:T(8,128)(2,1)} async-done(((bf16[8,768,384]{2,0,1:T(8,128)(2,1)}), bf16[8,768,384]{2,0,1:T(8,128)(2,1)}, u32[]{:S(2)}, u32[]{:S(2)}) %all-to-all-start.5) | async-done | bytes 4718624 | tf_op jit(solution)/shard_map/all_to_all | solution.py:188
  842.6 9.1 %copy.193 = f32[8,96,8,384]{3,2,1,0:T(8,128)} copy(f32[8,96,8,384]{3,0,1,2:T(8,128)S(1)} %convert_bitcast_fusion) | data formatting | bytes 18874368 | tf_op jit(solution)/shard_map/convert_element_type | solution.py:190
  851.7 11.0 %reshape.389 = f32[8,96,3072]{2,1,0:T(8,128)} reshape(f32[8,96,8,384]{3,2,1,0:T(8,128)} %copy.193) | data formatting | bytes 18874368 | tf_op jit(solution)/shard_map/convert_element_type | solution.py:190
  863.9 26.0 %reduce-scatter.10.cloned.1.call-done = bf16[24,3108]{1,0:T(8,128)(2,1)} async-done(((bf16[768,3108]{1,0:T(8,128)(2,1)}), bf16[24,3108]{1,0:T(8,128)(2,1)}) %reduce-scatter.10.cloned.1.call-update) | async-done | bytes 149200
  (205 shorter events, 133.0 us)
Async XLA Ops:
  7.2 71.9 %all-gather.4.cloned.1.call-start = ((), (), s32[]{:S(2)}) async-start(), calls=%async_computation.9 | async-start | bytes 5068800 | tf_op jit(solution)/shard_map/all_gather | solution.py:64
  11.9 314.6 %all-gather.6.cloned.1.call-start = ((), (), s32[]{:S(2)}) async-start(), calls=%async_computation.10 | async-start | bytes 5750784 | tf_op jit(solution)/shard_map/all_gather | solution.py:145
  22.3 61.9 %copy-start.19 = (f32[196]{0:T(256)}, f32[196]{0:T(256)S(1)}, u32[]{:S(2)}) copy-start(f32[196]{0:T(256)S(1)} %broadcast_multiply_fusion.1) | copy-start | bytes 2356
  23.5 60.7 %copy-start.24 = (f32[196]{0:T(256)}, f32[196]{0:T(256)S(1)}, u32[]{:S(2)}) copy-start(f32[196]{0:T(256)S(1)} %fusion.81) | copy-start | bytes 2356
  111.0 347.1 %reduce-scatter.6.cloned.1.call-start = ((), (), s32[]{:S(2)}) async-start(), calls=%async_computation.11 | async-start | bytes 5750784 | tf_op jit(solution)/shard_map/reduce_scatter | solution.py:152
  334.9 12.4 %copy-start.1 = (f32[8,416,384]{2,1,0:T(8,128)}, f32[8,416,384]{2,1,0:T(8,128)S(1)}, u32[]{:S(2)}) copy-start(f32[8,416,384]{2,1,0:T(8,128)S(1)} %get-tuple-element.109) | copy-start | bytes 15335428
  357.9 119.7 %copy-start.22 = (s32[1024]{0:T(1024)}, s32[1024]{0:T(1024)S(1)}, u32[]{:S(2)}) copy-start(s32[1024]{0:T(1024)S(1)} %pad_clamp_fusion.1) | copy-start | bytes 12292
  358.0 123.2 %copy-start.30 = (pred[196]{0:T(512)(128)(4,1)}, pred[196]{0:T(512)(128)(4,1)S(1)}, u32[]{:S(2)}) copy-start(pred[196]{0:T(512)(128)(4,1)S(1)} %get-tuple-element.112) | copy-start | bytes 592
  358.0 123.2 %copy-start.31 = (pred[196]{0:T(512)(128)(4,1)}, pred[196]{0:T(512)(128)(4,1)S(1)}, u32[]{:S(2)}) copy-start(pred[196]{0:T(512)(128)(4,1)S(1)} %get-tuple-element.113) | copy-start | bytes 592
  458.1 14.3 %all-to-all-start.2 = ((bf16[8,52,768]{2,0,1:T(8,128)(2,1)}), bf16[8,52,768]{2,0,1:T(8,128)(2,1)}, u32[]{:S(2)}, u32[]{:S(2)}) async-start(bf16[8,52,768]{2,0,1:T(8,128)(2,1)} %reduce-scatter.6.cloned.1.call-done), calls=%async_computation.3 | async-start | bytes 1277952 | tf_op jit(solution)/shard_map/all_to_all | solution.py:153
  462.3 124.5 %all-gather.8.cloned.1.call-start = ((), (), s32[]{:S(2)}) async-start(), calls=%async_computation.12 | async-start | bytes 5750784 | tf_op jit(solution)/shard_map/all_gather | solution.py:179
  462.5 16.9 %copy-start.23 = (s32[1024]{0:T(1024)}, s32[1024]{0:T(1024)S(1)}, u32[]{:S(2)}) copy-start(s32[1024]{0:T(1024)S(1)} %pad_clamp_fusion) | copy-start | bytes 12292
  463.6 6.2 copy-start.17
  503.6 205.7 %reduce-scatter.8.cloned.1.call-start = ((), (), s32[]{:S(2)}) async-start(), calls=%async_computation.13 | async-start | bytes 5750784 | tf_op jit(solution)/shard_map/reduce_scatter | solution.py:194
  597.6 6.9 copy-start.7
  709.3 15.7 %all-to-all-start.4 = ((bf16[8,52,768]{2,0,1:T(8,128)(2,1)}), bf16[8,52,768]{2,0,1:T(8,128)(2,1)S(1)}, u32[]{:S(2)}, u32[]{:S(2)}) async-start(bf16[8,52,768]{2,0,1:T(8,128)(2,1)} %reduce-scatter.8.cloned.1.call-done), calls=%async_computation.6 | async-start | bytes 1277952 | tf_op jit(solution)/shard_map/all_to_all | solution.py:195
  725.0 114.6 %all-to-all-start.5 = ((bf16[8,768,384]{2,0,1:T(8,128)(2,1)}), bf16[8,768,384]{2,0,1:T(8,128)(2,1)}, u32[]{:S(2)}, u32[]{:S(2)}) async-start(bf16[8,768,384]{2,0,1:T(8,128)(2,1)} %copy.192), calls=%async_computation.7 | async-start | bytes 9437184 | tf_op jit(solution)/shard_map/all_to_all | solution.py:188
  729.6 160.2 %reduce-scatter.10.cloned.1.call-start = ((), (), s32[]{:S(2)}) async-start(), calls=%async_computation.14 | async-start | bytes 5068800
  740.1 11.7 %copy-start.38 = (f32[12,196]{1,0:T(8,128)S(1)}, f32[12,196]{1,0:T(8,128)}, u32[]{:S(2)}) copy-start(f32[12,196]{1,0:T(8,128)} %copy-done.37) | copy-start | bytes 28228
  765.5 8.1 copy-start.12
  765.5 8.1 copy-start.14
  765.5 9.6 %copy-start.33 = (f32[768]{0:T(1024)S(1)}, f32[768]{0:T(1024)}, u32[]{:S(2)}) copy-start(f32[768]{0:T(1024)} %copy-done.32) | copy-start | bytes 9220
  851.7 11.0 %copy-start.4 = (bf16[196,768]{1,0:T(8,128)(2,1)S(1)}, bf16[196,768]{1,0:T(8,128)(2,1)}, u32[]{:S(2)}) copy-start(bf16[196,768]{1,0:T(8,128)(2,1)} %param.20) | copy-start | bytes 903172
  851.7 11.0 %copy-start.9 = (f32[196,768]{1,0:T(8,128)S(1)}, f32[196,768]{1,0:T(8,128)}, u32[]{:S(2)}) copy-start(f32[196,768]{1,0:T(8,128)} %copy-done.8) | copy-start | bytes 1806340
  (24 other events, 69.5 us)
Sparse Core Ops, SparseCore 0:
  12.0 66.9 all-gather.3
  111.1 163.1 all-gather.5
  358.0 100.0 reduce-scatter.5
  503.7 82.9 all-gather.7
  609.9 99.3 reduce-scatter.7
  787.1 102.6 reduce-scatter.9
where the time goes:
time: 912 us; the launch traced here: 903 us
  waiting for transfers between devices  406 us (45%)
  blocking collectives  227 us (25%)
  local copies, waits for them, and re-layouts  119 us (13%)
  matrix products  88.4 us (10%)
  other arithmetic  33.1 us (4%)
  between operations  16.5 us (2%)
  starting transfers between devices  13.3 us (1%)
    all_to_all x1, blocking collectives, body(): lax.all_to_all(w_up, 'dp', split_axis=2, concat_axis=1, tiled=True)  198 us
    reduce_scatter x1, waiting for transfers between devices, body(): produced = lax.psum_scatter(produced, 'dp', scatter_dimension=1, tiled=True)  100 us
    reduce_scatter x1, waiting for transfers between devices, body(): lax.psum_scatter(input_grad, 'dp', scatter_dimension=1, tiled=True)  96.9 us
    all_gather x1, waiting for transfers between devices, body(): grad_arrived = lax.all_gather(grad_arrived, 'dp', axis=1, tiled=True)  83.1 us
    all_gather x1, waiting for transfers between devices, body(): lax.all_gather(jnp.concatenate([w_qkv, w_out, w_router] + [vector[:, None...  55 us
    all_to_all x1, waiting for transfers between devices, body(): lax.all_to_all(up_grad.astype(jnp.bfloat16), 'dp', split_axis=1, concat_a...  43.3 us
    unnamed x7, waiting for transfers between devices  26.1 us
    convert_element_type x2, local copies, waits for them, and re-layouts, body(): up_share = lax.all_to_all(up_grad.astype(jnp.bfloat16), 'dp', split_axis=...  20.1 us
  transfers between devices with their start and end apart: 9, of which 7 were waited for; matrix products, arithmetic and copies ran while one was open for 15% of the time, Pallas kernels for 0%

commit v1 on v0

--- a/solution.py
+++ b/solution.py
@@ -12,6 +12,18 @@
 PATCH_S = 49
 PATCH_L = 196
 CAP = 13
+
+
+def gather_by_bits(shard, axis, dim):
+    ways, here, step = (lax.axis_size(axis), lax.axis_index(axis), shard.shape[dim])
+    line, have = (shard, 1)
+    while have < ways:
+        line = jnp.concatenate(
+            [line, lax.ppermute(line, axis, [(d, (d - have) % ways) for d in range(ways)])],
+            axis=dim,
+        )
+        have = 2 * have
+    return jnp.roll(line, here * step, axis=dim)
 
 
 def normalize(inputs, scale_vec, shift_vec):
@@ -176,7 +188,7 @@
     grad_arrived = lax.all_to_all(
         grad_send.reshape(EXPERTS, CAP, D), "expert", split_axis=0, concat_axis=1, tiled=True
     )
-    grad_arrived = lax.all_gather(grad_arrived, "dp", axis=1, tiled=True)
+    grad_arrived = gather_by_bits(grad_arrived, "dp", 1)
     down_share = jnp.einsum(
         "erf,erd->efd", activated, grad_arrived, preferred_element_type=jnp.float32
     )

time: 912 us -> 1050 us (1.15)
  waiting for transfers between devices: 406 us -> 478 us
  local copies, waits for them, and re-layouts: 119 us -> 177 us
    ppermute x0 -> x3, waiting for transfers between devices: none -> 150 us  [gather_by_bits(): lax.ppermute(line, axis, [(d, (d - have) % ways) for d in range(ways)])]
    all_gather x1 -> x0, waiting for transfers between devices: 83.1 us -> none  [body(): grad_arrived = lax.all_gather(grad_arrived, 'dp', axis=1, tiled=True)]
    concatenate x0 -> x1, local copies, waits for them, and re-layouts: none -> 60.6 us  [gather_by_bits(): return jnp.roll(line, here * step, axis=dim)]
    unnamed x7 -> x6, waiting for transfers between devices: 26.1 us -> 23.3 us
  transfers between devices with their start and end apart: 9 -> 11, of which waited for: 7 -> 9; matrix products, arithmetic and copies ran while one was open for 15% -> 13% of each run, Pallas kernels for 0% -> 0%
where the time goes in v1:
time: 1050 us; the launch traced here: 1040 us
  waiting for transfers between devices  478 us (46%)
  blocking collectives  227 us (22%)
  local copies, waits for them, and re-layouts  177 us (17%)
  matrix products  84.8 us (8%)
  other arithmetic  33.9 us (3%)
  starting transfers between devices  19.8 us (2%)
  between operations  16.2 us (2%)
    all_to_all x1, blocking collectives, body(): lax.all_to_all(w_up, 'dp', split_axis=2, concat_axis=1, tiled=True)  198 us
    ppermute x3, waiting for transfers between devices, gather_by_bits(): lax.ppermute(line, axis, [(d, (d - have) % ways) for d in range(ways)])  150 us
    reduce_scatter x1, waiting for transfers between devices, body(): lax.psum_scatter(input_grad, 'dp', scatter_dimension=1, tiled=True)  101 us
    reduce_scatter x1, waiting for transfers between devices, body(): produced = lax.psum_scatter(produced, 'dp', scatter_dimension=1, tiled=True)  100 us
    concatenate x1, local copies, waits for them, and re-layouts, gather_by_bits(): return jnp.roll(line, here * step, axis=dim)  60.6 us
    all_gather x1, waiting for transfers between devices, body(): lax.all_gather(jnp.concatenate([w_qkv, w_out, w_router] + [vector[:, None...  55 us
    all_to_all x1, waiting for transfers between devices, body(): lax.all_to_all(up_grad.astype(jnp.bfloat16), 'dp', split_axis=1, concat_a...  46.4 us
    unnamed x6, waiting for transfers between devices  23.3 us
  transfers between devices with their start and end apart: 11, of which 9 were waited for; matrix products, arithmetic and copies ran while one was open for 13% of the time, Pallas kernels for 0%

profile of v1, /device:TPU:0, one launch (start us, length us, event | category | flops | bytes accessed | tf_op | source)
XLA Modules:
  0.0 1036.3 jit_solution(12861683037534244128)
XLA Ops:
  24.1 55.0 %all-gather.3.cloned.1.call-done = bf16[768,3108]{1,0:T(8,128)(2,1)} async-done(((bf16[24,3108]{1,0:T(8,128)(2,1)}), bf16[768,3108]{1,0:T(8,128)(2,1)}) %all-gather.3.cloned.1.call-update) | async-done | bytes 4773904 | tf_op jit(solution)/shard_map/all_gather | solution.py:76
  94.9 14.2 %all_to_all.93 = bf16[32,13,768]{2,1,0:T(8,128)(2,1)S(1)} all-to-all(bf16[32,13,768]{2,1,0:T(8,128)(2,1)S(1)} %broadcast_select_fusion), channel_id=1, replica_groups=mesh['dp'=8,'expert'=4] {'expert'}, dimensions={0} | all-to-all | bytes 1277952 | tf_op jit(solution)/shard_map/all_to_all | solution.py:156
  110.2 8.6 copy.186
  118.8 198.4 %all_to_all.94 = bf16[8,96,3072]{1,0,2:T(8,128)(2,1)} all-to-all(bf16[8,96,3072]{1,0,2:T(8,128)(2,1)} %copy.186), channel_id=1, replica_groups=mesh['dp'=8,'expert'=4] {'dp'}, dimensions={2} | all-to-all | bytes 9437184 | tf_op jit(solution)/shard_map/all_to_all | solution.py:93
  317.2 8.5 copy.187
  325.7 8.5 fusion.35
  334.3 12.4 %multiply_convert_fusion = (bf16[8,416,384]{2,1,0:T(8,128)(2,1)S(1)}, f32[8,416,384]{2,1,0:T(8,128)}) fusion(f32[8,416,384]{2,1,0:T(8,128)S(1)} %get-tuple-element.109, u8[416,384]{1,0:T(8,128)(4,1)S(1)} %get-tuple-element.54, u8[416,384]{1,0:T(8,128)(4,1)S(1)} %get-tuple-element.53), kind=kLoop, calls=%fused_computation.19 | loop fusion | flops 89456640 | bytes 13099008 | tf_op jit(solution)/shard_map/convert_element_type | solution.py:160
  355.0 100.1 %reduce-scatter.6.cloned.1.call-done = bf16[8,52,768]{2,0,1:T(8,128)(2,1)} async-done(((bf16[8,416,768]{2,0,1:T(8,128)(2,1)}), bf16[8,52,768]{2,0,1:T(8,128)(2,1)}) %reduce-scatter.6.cloned.1.call-update) | async-done | bytes 638992 | tf_op jit(solution)/shard_map/reduce_scatter | solution.py:164
  484.8 14.0 %all_to_all.95 = bf16[32,13,768]{2,1,0:T(8,128)(2,1)S(1)} all-to-all(bf16[32,13,768]{2,1,0:T(8,128)(2,1)S(1)} %multiply_convert_fusion.2), channel_id=1, replica_groups=mesh['dp'=8,'expert'=4] {'expert'}, dimensions={0} | all-to-all | bytes 1277952 | tf_op jit(solution)/shard_map/all_to_all | solution.py:188
  502.2 13.2 %collective-permute-done = bf16[8,52,768]{2,0,1:T(8,128)(2,1)S(1)} collective-permute-done((bf16[8,52,768]{2,0,1:T(8,128)(2,1)S(1)}, bf16[8,52,768]{2,0,1:T(8,128)(2,1)S(1)}, u32[]{:S(2)}, u32[]{:S(2)}) %collective-permute-start) | collective-permute-done | bytes 639008 | tf_op jit(solution)/shard_map/ppermute | solution.py:22
  517.5 27.0 %collective-permute-done.1 = bf16[8,104,768]{2,1,0:T(8,128)(2,1)S(1)} collective-permute-done((bf16[8,104,768]{2,1,0:T(8,128)(2,1)S(1)}, bf16[8,104,768]{2,1,0:T(8,128)(2,1)S(1)}, u32[]{:S(2)}, u32[]{:S(2)}) %collective-permute-start.1) | collective-permute-done | bytes 1277984 | tf_op jit(solution)/shard_map/ppermute | solution.py:22
  548.1 109.5 %collective-permute-done.2 = bf16[8,208,768]{2,1,0:T(8,128)(2,1)} collective-permute-done((bf16[8,208,768]{2,1,0:T(8,128)(2,1)}, bf16[8,208,768]{2,1,0:T(8,128)(2,1)}, u32[]{:S(2)}, u32[]{:S(2)}) %collective-permute-start.2) | collective-permute-done | bytes 2555936 | tf_op jit(solution)/shard_map/ppermute | solution.py:22
  657.6 60.6 %concatenate.47 = bf16[8,832,768]{2,1,0:T(8,128)(2,1)} concatenate(bf16[8,52,768]{2,1,0:T(8,128)(2,1)} %copy-done, bf16[8,52,768]{2,1,0:T(8,128)(2,1)} %copy-done.1, bf16[8,104,768]{2,1,0:T(8,128)(2,1)} %copy-done.2, bf16[8,208,768]{2,1,0:T(8,128)(2,1)} %collective-permute-done.2, bf16[8,52,768]{2,1,0:T(8,128)(2,1)} %copy-done, bf16[8,52,768]{2,1,0:T(8,128)(2,1)} %copy-done.1, ...), dimensions={1} | concatenate | bytes 20447232 | tf_op jit(solution)/shard_map/jit(_roll_dynamic)/concatenate | solution.py:26
  718.2 12.3 %add_convert_fusion = bf16[8,416,384]{2,1,0:T(8,128)(2,1)} fusion(f32[8,416,384]{2,1,0:T(8,128)} %get-tuple-element.90, f32[8,416,384]{2,1,0:T(8,128)} %copy-done.4, bf16[8,384,768]{2,1,0:T(8,128)(2,1)} %param.29, bf16[8,832,768]{2,1,0:T(8,128)(2,1)} %concatenate.47, s32[]{:T(128)S(6)} %select_n.113), kind=kOutput, calls=%fused_computation.18 | convolution fusion | flops 1980825600 | bytes 22609924 | tf_op jit(solution)/shard_map/erd,efd->erf/dot_general | solution.py:195
  742.9 100.8 %reduce-scatter.8.cloned.1.call-done = bf16[8,52,768]{2,0,1:T(8,128)(2,1)} async-done(((bf16[8,416,768]{2,0,1:T(8,128)(2,1)}), bf16[8,52,768]{2,0,1:T(8,128)(2,1)}) %reduce-scatter.8.cloned.1.call-update) | async-done | bytes 638992 | tf_op jit(solution)/shard_map/reduce_scatter | solution.py:206
  847.6 6.8 fusion.19
  887.1 5.6 fusion.36
  892.7 5.6 fusion.39
  911.9 8.7 concatenate.50
  920.6 8.9 fusion.12
  929.5 46.4 %all-to-all-done.5 = bf16[8,768,384]{2,0,1:T(8,128)(2,1)} async-done(((bf16[8,768,384]{2,0,1:T(8,128)(2,1)}), bf16[8,768,384]{2,0,1:T(8,128)(2,1)}, u32[]{:S(2)}, u32[]{:S(2)}) %all-to-all-start.5) | async-done | bytes 4718624 | tf_op jit(solution)/shard_map/all_to_all | solution.py:200
  979.1 9.1 copy.216
  988.2 11.0 %reshape.389 = f32[8,96,3072]{2,1,0:T(8,128)} reshape(f32[8,96,8,384]{3,2,1,0:T(8,128)} %copy.216) | data formatting | bytes 18874368 | tf_op jit(solution)/shard_map/convert_element_type | solution.py:202
  1000.3 23.2 %reduce-scatter.10.cloned.1.call-done = bf16[24,3108]{1,0:T(8,128)(2,1)} async-done(((bf16[768,3108]{1,0:T(8,128)(2,1)}), bf16[24,3108]{1,0:T(8,128)(2,1)}) %reduce-scatter.10.cloned.1.call-update) | async-done | bytes 149200
  (227 shorter events, 151.5 us)
Async XLA Ops:
  7.2 71.9 %all-gather.3.cloned.1.call-start = ((), (), s32[]{:S(2)}) async-start(), calls=%async_computation.9 | async-start | bytes 5068800 | tf_op jit(solution)/shard_map/all_gather | solution.py:76
  11.9 313.8 %all-gather.5.cloned.1.call-start = ((), (), s32[]{:S(2)}) async-start(), calls=%async_computation.10 | async-start | bytes 5750784 | tf_op jit(solution)/shard_map/all_gather | solution.py:157
  17.5 66.6 %copy-start.36 = (s32[392,1]{0,1:T(1,128)}, s32[392,1]{0,1:T(1,128)S(1)}, u32[]{:S(2)}) copy-start(s32[392,1]{0,1:T(1,128)S(1)} %compare_select_fusion.1) | copy-start | bytes 4708
  22.3 61.8 %copy-start.21 = (f32[196]{0:T(256)}, f32[196]{0:T(256)S(1)}, u32[]{:S(2)}) copy-start(f32[196]{0:T(256)S(1)} %broadcast_multiply_fusion.1) | copy-start | bytes 2356
  23.5 60.6 %copy-start.26 = (f32[196]{0:T(256)}, f32[196]{0:T(256)S(1)}, u32[]{:S(2)}) copy-start(f32[196]{0:T(256)S(1)} %fusion.81) | copy-start | bytes 2356
  92.2 16.8 %copy-start.8 = (bf16[196,768]{1,0:T(8,128)(2,1)}, bf16[196,768]{1,0:T(8,128)(2,1)S(1)}, u32[]{:S(2)}) copy-start(bf16[196,768]{1,0:T(8,128)(2,1)S(1)} %add_convert_fusion.1) | copy-start | bytes 903172
  110.1 345.0 %reduce-scatter.6.cloned.1.call-start = ((), (), s32[]{:S(2)}) async-start(), calls=%async_computation.11 | async-start | bytes 5750784 | tf_op jit(solution)/shard_map/reduce_scatter | solution.py:164
  317.2 29.5 %slice-start.2 = ((s8[4718592]{0:T(1024)(128)(4,1)}), s8[524288]{0:T(1024)(128)(4,1)S(1)}, s32[]{:S(2)}) async-start(s8[4718592]{0:T(1024)(128)(4,1)} %bitcast.90), calls=%async_computation.16 | async-start | bytes 1048576
  325.7 21.0 %slice-start.3 = ((s8[4718592]{0:T(1024)(128)(4,1)}), s8[4194304]{0:T(1024)(128)(4,1)S(1)}, s32[]{:S(2)}) async-start(s8[4718592]{0:T(1024)(128)(4,1)} %bitcast.90), calls=%async_computation.17 | async-start | bytes 8388608
  354.9 119.7 %copy-start.24 = (s32[1024]{0:T(1024)}, s32[1024]{0:T(1024)S(1)}, u32[]{:S(2)}) copy-start(s32[1024]{0:T(1024)S(1)} %pad_clamp_fusion) | copy-start | bytes 12292
  355.0 123.2 %copy-start.32 = (pred[196]{0:T(512)(128)(4,1)}, pred[196]{0:T(512)(128)(4,1)S(1)}, u32[]{:S(2)}) copy-start(pred[196]{0:T(512)(128)(4,1)S(1)} %get-tuple-element.112) | copy-start | bytes 592
  355.0 123.2 %copy-start.33 = (pred[196]{0:T(512)(128)(4,1)}, pred[196]{0:T(512)(128)(4,1)S(1)}, u32[]{:S(2)}) copy-start(pred[196]{0:T(512)(128)(4,1)S(1)} %get-tuple-element.113) | copy-start | bytes 592
  455.1 14.3 %all-to-all-start.2 = ((bf16[8,52,768]{2,0,1:T(8,128)(2,1)}), bf16[8,52,768]{2,0,1:T(8,128)(2,1)}, u32[]{:S(2)}, u32[]{:S(2)}) async-start(bf16[8,52,768]{2,0,1:T(8,128)(2,1)} %reduce-scatter.6.cloned.1.call-done), calls=%async_computation.3 | async-start | bytes 1277952 | tf_op jit(solution)/shard_map/all_to_all | solution.py:165
  459.2 384.4 %reduce-scatter.8.cloned.1.call-start = ((), (), s32[]{:S(2)}) async-start(), calls=%async_computation.12 | async-start | bytes 5750784 | tf_op jit(solution)/shard_map/reduce_scatter | solution.py:206
  459.5 16.9 %copy-start.25 = (s32[1024]{0:T(1024)}, s32[1024]{0:T(1024)S(1)}, u32[]{:S(2)}) copy-start(s32[1024]{0:T(1024)S(1)} %pad_clamp_fusion.1) | copy-start | bytes 12292
  499.1 16.3 %collective-permute-start = (bf16[8,52,768]{2,0,1:T(8,128)(2,1)S(1)}, bf16[8,52,768]{2,0,1:T(8,128)(2,1)S(1)}, u32[]{:S(2)}, u32[]{:S(2)}) collective-permute-start(bf16[8,52,768]{2,0,1:T(8,128)(2,1)S(1)} %bitcast.96), channel_id=1, source_target_pairs={{0,28},{4,0},{8,4},{12,8},{16,12},{20,16},{24,20},{28,24},{1,29},{... | collective-permute-start | bytes 1916936 | tf_op jit(solution)/shard_map/ppermute | solution.py:22
  502.2 42.4 %copy-start = (bf16[8,52,768]{2,1,0:T(8,128)(2,1)}, bf16[8,52,768]{2,1,0:T(8,128)(2,1)S(1)}, u32[]{:S(2)}) copy-start(bf16[8,52,768]{2,1,0:T(8,128)(2,1)S(1)} %copy.198) | copy-start | bytes 1916932
  515.5 31.0 %copy-start.1 = (bf16[8,52,768]{2,1,0:T(8,128)(2,1)}, bf16[8,52,768]{2,1,0:T(8,128)(2,1)S(1)}, u32[]{:S(2)}) copy-start(bf16[8,52,768]{2,1,0:T(8,128)(2,1)S(1)} %copy.199) | copy-start | bytes 1916932
  515.7 28.9 %collective-permute-start.1 = (bf16[8,104,768]{2,1,0:T(8,128)(2,1)S(1)}, bf16[8,104,768]{2,1,0:T(8,128)(2,1)S(1)}, u32[]{:S(2)}, u32[]{:S(2)}) collective-permute-start(bf16[8,104,768]{2,1,0:T(8,128)(2,1)S(1)} %pad_maximum_fusion.1), channel_id=1, source_target_pairs={{0,24},{4,28},{8,0},{12,4},{16,8},{20,12},{24,16},{28,20},{1,25},{... | collective-permute-start | bytes 3833864 | tf_op jit(solution)/shard_map/ppermute | solution.py:22
  546.5 111.1 %collective-permute-start.2 = (bf16[8,208,768]{2,1,0:T(8,128)(2,1)}, bf16[8,208,768]{2,1,0:T(8,128)(2,1)}, u32[]{:S(2)}, u32[]{:S(2)}) collective-permute-start(bf16[8,208,768]{2,1,0:T(8,128)(2,1)} %pad_maximum_fusion), channel_id=1, source_target_pairs={{0,16},{4,20},{8,24},{12,28},{16,0},{20,4},{24,8},{28,12},{1,17},{... | collective-permute-start | bytes 7667720 | tf_op jit(solution)/shard_map/ppermute | solution.py:22
  657.6 72.9 %slice-start = ((s8[4718592]{0:T(1024)(128)(4,1)}), s8[524288]{0:T(1024)(128)(4,1)S(1)}, s32[]{:S(2)}) async-start(s8[4718592]{0:T(1024)(128)(4,1)} %bitcast.87), calls=%async_computation.14 | async-start | bytes 1048576
  843.7 15.8 %all-to-all-start.4 = ((bf16[8,52,768]{2,0,1:T(8,128)(2,1)}), bf16[8,52,768]{2,0,1:T(8,128)(2,1)S(1)}, u32[]{:S(2)}, u32[]{:S(2)}) async-start(bf16[8,52,768]{2,0,1:T(8,128)(2,1)} %reduce-scatter.8.cloned.1.call-done), calls=%async_computation.6 | async-start | bytes 1277952 | tf_op jit(solution)/shard_map/all_to_all | solution.py:207
  859.5 116.5 %all-to-all-start.5 = ((bf16[8,768,384]{2,0,1:T(8,128)(2,1)}), bf16[8,768,384]{2,0,1:T(8,128)(2,1)}, u32[]{:S(2)}, u32[]{:S(2)}) async-start(bf16[8,768,384]{2,0,1:T(8,128)(2,1)} %copy.215), calls=%async_computation.7 | async-start | bytes 9437184 | tf_op jit(solution)/shard_map/all_to_all | solution.py:200
  864.1 159.5 %reduce-scatter.10.cloned.1.call-start = ((), (), s32[]{:S(2)}) async-start(), calls=%async_computation.13 | async-start | bytes 5068800
  (32 other events, 149.9 us)
Sparse Core Ops, SparseCore 0:
  12.0 66.9 all-gather.2
  110.2 163.1 all-gather.4
  355.0 100.0 reduce-scatter.5
  740.4 103.2 reduce-scatter.7
  920.7 102.7 reduce-scatter.9
